TPU v7x, 32 devices: a whole 2x2x4 slice. The times are simulated.
32 devices in a mesh: lon: 4 (over y, x), lat: 4 (over z), mem: 2 (over core).
Axes of the slice: x: 2, y: 2, z: 4, core: 2. Of those that a mesh axis runs over, the one named last changes fastest.
Arguments:
- north_vel: bfloat16 [2, 4, 75, 128, 512], P('mem', None, None, 'lat', 'lon'), may hold values from -6 to 6
- up_vel: bfloat16 [2, 4, 75, 128, 512], P('mem', None, None, 'lat', 'lon'), may hold values from -6 to 6
- dens_class: int32 [2, 4, 75, 128, 512], P('mem', None, None, 'lat', 'lon'), may hold values from 0 to 79
- thickness: int32 [75, 128, 512], P(None, 'lat', 'lon'), may hold values from 0 to 2000
- basin_id: int32 [128, 512], P('lat', 'lon'), may hold values from 0 to 3
Outputs:
- depth_mean: float32 [4, 4, 2, 75, 128], P('lon', None, None, None, 'lat')
- depth_spread: float32 [4, 4, 2, 75, 128], P('lon', None, None, None, 'lat')
- class_mean: float32 [4, 4, 2, 80, 128], P('lon', None, None, None, 'lat')
- class_spread: float32 [4, 4, 2, 80, 128], P('lon', None, None, None, 'lat')
Inputs may be any that keep to these rules, and one draw needn't show every extreme that they name: `basin_id`: 0 marks land; 1 to 3 name the basins. `thickness`: thousandths of a unit layer; 0 marks a cell below the sea floor.
All inputs are finite; a program needn't handle non-finite values.
Results may differ from a plain program's by a relative error of at most 0.0029.
Values sent between devices are 32-bit elements; how exact they have to be, the bound alone decides.
A program may use at most 128 MiB of HBM per device.

v0:
```python
import math

import jax
import jax.numpy as jnp
from jax import lax
from jax.sharding import PartitionSpec as P

CLASSES = 80
BASINS = 3


north_unit = 0.02
up_unit = 0.01


def carried_in(shard, axis, combine, identity):
    devices, mine = (lax.axis_size(axis), lax.axis_index(axis))
    everything = jax.tree.map(lambda part: lax.all_gather(part, axis), shard)
    start = jax.tree.map(
        lambda part, zero: jnp.broadcast_to(jnp.asarray(zero, part.dtype), part.shape),
        shard,
        identity,
    )

    def lap(k, before):
        reached = k < mine
        new = combine(before, jax.tree.map(lambda part: part[k], everything))
        return jax.tree.map(lambda a, b: jnp.where(reached, a, b), new, before)

    return lax.fori_loop(0, devices, lap, start)


def class_sums(north_flux, rise_flux, dens_class, basin_id):
    months, levels, lat_rows, lon_cells = north_flux.shape
    block = 1
    for cand in range(16, 0, -1):
        if levels % cand == 0:
            block = cand
            break
    turns = months * (levels // block)
    weighted = jnp.stack([north_flux, rise_flux], 1).reshape(
        months, 2, levels // block, block, lat_rows, lon_cells
    )
    weighted = jnp.moveaxis(weighted, 2, 1).reshape(turns, 2, block, lat_rows, lon_cells)
    combined = jnp.where(
        basin_id[None, None] > 0, (basin_id[None, None] - 1) * CLASSES + dens_class, -1
    )
    combined = combined.reshape(turns, block, lat_rows, lon_cells)
    column_ids = jnp.arange(BASINS * CLASSES, dtype=jnp.int32)

    def one_block(packed):
        onehot = (packed[1][..., None] == column_ids).astype(jnp.bfloat16)
        return jnp.einsum("skji,kjiq->sqj", packed[0], onehot, preferred_element_type=jnp.float32)

    per_block = lax.map(one_block, (weighted, combined))
    per_block = per_block.reshape(months, levels // block, 2, BASINS, CLASSES, lat_rows)
    return jnp.swapaxes(jnp.sum(per_block, axis=1), 1, 2)


def local_tables(north_vel, up_vel, dens_class, thickness, basin_id, first_row, lat_total):
    months, levels, lat_rows, lon_cells = north_vel.shape
    row_index = first_row + jnp.arange(lat_rows, dtype=jnp.int32)
    latitude = (-78.0 + 156.0 * (row_index.astype(jnp.float32) + 0.5) / lat_total) * (
        math.pi / 180.0
    )
    zonal_width = jnp.cos(latitude)
    layer_depth = thickness.astype(jnp.float32) * 0.001
    wet_cells = (thickness > 0).astype(jnp.float32)
    north_flux = (
        north_vel.astype(jnp.float32)
        * (north_unit * zonal_width)[None, None, :, None]
        * layer_depth[None]
    ).astype(jnp.bfloat16)
    rise_flux = (
        up_vel.astype(jnp.float32) * (up_unit * zonal_width)[None, None, :, None] * wet_cells[None]
    ).astype(jnp.bfloat16)
    basin_masks = (
        basin_id[None] == jnp.arange(1, BASINS + 1, dtype=jnp.int32)[:, None, None]
    ).astype(jnp.bfloat16)
    north_depth = jnp.einsum(
        "mkji,bji->mbkj", north_flux, basin_masks, preferred_element_type=jnp.float32
    )
    rise_depth = jnp.einsum(
        "mkji,bji->mbkj", rise_flux, basin_masks, preferred_element_type=jnp.float32
    )
    depth_tab = jnp.stack([north_depth, rise_depth], 2)
    class_tab = class_sums(north_flux, rise_flux, dens_class, basin_id)
    return (class_tab, depth_tab)


def with_global(tables):
    return jnp.concatenate([jnp.sum(tables, axis=2, keepdims=True), tables], 2)


def add_pair(earlier, latter):
    return (earlier[0] + latter[0], earlier[1] + latter[1])


def body(north_vel, up_vel, dens_class, thickness, basin_id):
    row_count = north_vel.shape[3]
    first_row = lax.axis_index("lat") * row_count
    lat_total = row_count * lax.axis_size("lat")

    def one_member(packed):
        return local_tables(
            packed[0], packed[1], packed[2], thickness, basin_id, first_row, lat_total
        )

    class_tab, depth_tab = lax.map(one_member, (north_vel, up_vel, dens_class))
    class_tab, depth_tab = (
        lax.psum_scatter(class_tab, "lon", scatter_dimension=1, tiled=True),
        lax.psum_scatter(depth_tab, "lon", scatter_dimension=1, tiled=True),
    )
    class_reg = with_global(class_tab)
    depth_reg = with_global(depth_tab)
    class_block = jnp.sum(class_reg[:, :, :, 1], axis=-1)
    depth_block = jnp.sum(depth_reg[:, :, :, 1], axis=-1)
    carry_class, carry_depth = carried_in(
        (class_block, depth_block),
        "lat",
        add_pair,
        (jnp.zeros_like(class_block), jnp.zeros_like(depth_block)),
    )
    class_south = jnp.cumsum(class_reg[:, :, :, 1], axis=4) + carry_class[..., None]
    class_moc = jnp.stack(
        [jnp.cumsum(class_reg[:, :, :, 0], axis=3), jnp.cumsum(class_south, axis=3)], 3
    )
    depth_south = jnp.cumsum(depth_reg[:, :, :, 1], axis=4) + carry_depth[..., None]
    depth_moc = jnp.stack([jnp.cumsum(depth_reg[:, :, :, 0], axis=3), depth_south], 3)
    members = class_moc.shape[0] * lax.axis_size("mem")
    class_total, depth_total = lax.psum((jnp.sum(class_moc, 0), jnp.sum(depth_moc, 0)), "mem")
    class_mean = class_total / members
    depth_mean = depth_total / members
    class_dev, depth_dev = lax.psum(
        (
            jnp.sum(jnp.square(class_moc - class_mean), 0),
            jnp.sum(jnp.square(depth_moc - depth_mean), 0),
        ),
        "mem",
    )
    class_spread = jnp.sqrt(class_dev / (members - 1))
    depth_spread = jnp.sqrt(depth_dev / (members - 1))
    return (depth_mean, depth_spread, class_mean, class_spread)


def solution(mesh):
    in_specs = (
        P("mem", None, None, "lat", "lon"),
        P("mem", None, None, "lat", "lon"),
        P("mem", None, None, "lat", "lon"),
        P(None, "lat", "lon"),
        P("lat", "lon"),
    )
    out_specs = (
        P("lon", None, None, None, "lat"),
        P("lon", None, None, None, "lat"),
        P("lon", None, None, None, "lat"),
        P("lon", None, None, None, "lat"),
    )
    return jax.shard_map(body, mesh=mesh, in_specs=in_specs, out_specs=out_specs, check_vma=False)
```

profile of v0, /device:TPU:0, one launch (start us, length us, event | category | flops | bytes accessed | tf_op | source)
XLA Modules:
  0.0 399.0 jit_solution(3414294359119029780)
XLA Ops:
  9.1 3.1 fusion.7
  18.0 2.9 fusion.10
  21.2 2.1 fusion.16
  23.4 2.3 fusion.30
  30.3 5.4 %add_select_fusion.2 = s32[20,15,32,128]{3,2,1,0:T(8,128)} fusion(s32[20,15,32,128]{3,2,1,0:T(8,128)} %bitcast.116, s32[32,128]{1,0:T(8,128)S(1)} %add_multiply_fusion, pred[32,128]{1,0:T(8,128)(4,1)S(1)} %broadcast_compare_fusion), kind=kLoop, calls=%fused_computation.36 | loop fusion | flops 2457600 | bytes 9850880 | tf_op jit(solution)/shard_map/while/body/eval_jaxpr/jit(_where)/select_n | solution.py:45
  35.8 263.9 %while.35 = (s32[]{:T(128)}, f32[20,2,240,32]{2,3,1,0:T(8,128)}, s32[20,15,32,128]{3,2,1,0:T(8,128)}, bf16[20,2,15,32,128]{4,3,2,1,0:T(8,128)(2,1)}, s32[]{:T(128)}) while((s32[]{:T(128)}, f32[20,2,240,32]{2,3,1,0:T(8,128)}, s32[20,15,32,128]{3,2,1,0:T(8,128)}, bf16[20,2,15,32,128]{4,3,2,1,0:T(8,128)(2,1)}, s32[]{:T(128)}) %tuple.66), condition=%wide.region_5.6_spmd.clone, body=%wide.region_4.5_spmd.clone.sunk | while | flops 73728000 | bytes 2155077 | solution.py:55
  37.8 10.5 %fusion.53 = f32[1,2,240,32]{2,1,3,0:T(2,128)S(1)} fusion(s32[15,32,128]{2,0,1:T(8,128)S(1)} %bitcast.115, bf16[1,2,15,32,128]{4,3,2,1,0:T(8,128)(2,1)S(1)} %constant_dynamic-slice_fusion.5), kind=kOutput, calls=%fused_computation.4.clone.1 | convolution fusion | flops 73728000 | bytes 552960 | tf_op jit(solution)/shard_map/while/body/eval_jaxpr/while/body/eval_jaxpr/skji,kjiq->sqj/dot_general | solution.py:53
  51.0 10.5 %fusion.53 = f32[1,2,240,32]{2,1,3,0:T(2,128)S(1)} fusion(s32[15,32,128]{2,0,1:T(8,128)S(1)} %bitcast.115, bf16[1,2,15,32,128]{4,3,2,1,0:T(8,128)(2,1)S(1)} %constant_dynamic-slice_fusion.5), kind=kOutput, calls=%fused_computation.4.clone.1 | convolution fusion | flops 73728000 | bytes 552960 | tf_op jit(solution)/shard_map/while/body/eval_jaxpr/while/body/eval_jaxpr/skji,kjiq->sqj/dot_general | solution.py:53
  64.2 10.5 %fusion.53 = f32[1,2,240,32]{2,1,3,0:T(2,128)S(1)} fusion(s32[15,32,128]{2,0,1:T(8,128)S(1)} %bitcast.115, bf16[1,2,15,32,128]{4,3,2,1,0:T(8,128)(2,1)S(1)} %constant_dynamic-slice_fusion.5), kind=kOutput, calls=%fused_computation.4.clone.1 | convolution fusion | flops 73728000 | bytes 552960 | tf_op jit(solution)/shard_map/while/body/eval_jaxpr/while/body/eval_jaxpr/skji,kjiq->sqj/dot_general | solution.py:53
  77.4 10.5 %fusion.53 = f32[1,2,240,32]{2,1,3,0:T(2,128)S(1)} fusion(s32[15,32,128]{2,0,1:T(8,128)S(1)} %bitcast.115, bf16[1,2,15,32,128]{4,3,2,1,0:T(8,128)(2,1)S(1)} %constant_dynamic-slice_fusion.5), kind=kOutput, calls=%fused_computation.4.clone.1 | convolution fusion | flops 73728000 | bytes 552960 | tf_op jit(solution)/shard_map/while/body/eval_jaxpr/while/body/eval_jaxpr/skji,kjiq->sqj/dot_general | solution.py:53
  90.6 10.5 %fusion.53 = f32[1,2,240,32]{2,1,3,0:T(2,128)S(1)} fusion(s32[15,32,128]{2,0,1:T(8,128)S(1)} %bitcast.115, bf16[1,2,15,32,128]{4,3,2,1,0:T(8,128)(2,1)S(1)} %constant_dynamic-slice_fusion.5), kind=kOutput, calls=%fused_computation.4.clone.1 | convolution fusion | flops 73728000 | bytes 552960 | tf_op jit(solution)/shard_map/while/body/eval_jaxpr/while/body/eval_jaxpr/skji,kjiq->sqj/dot_general | solution.py:53
  103.8 10.5 %fusion.53 = f32[1,2,240,32]{2,1,3,0:T(2,128)S(1)} fusion(s32[15,32,128]{2,0,1:T(8,128)S(1)} %bitcast.115, bf16[1,2,15,32,128]{4,3,2,1,0:T(8,128)(2,1)S(1)} %constant_dynamic-slice_fusion.5), kind=kOutput, calls=%fused_computation.4.clone.1 | convolution fusion | flops 73728000 | bytes 552960 | tf_op jit(solution)/shard_map/while/body/eval_jaxpr/while/body/eval_jaxpr/skji,kjiq->sqj/dot_general | solution.py:53
  117.0 10.5 %fusion.53 = f32[1,2,240,32]{2,1,3,0:T(2,128)S(1)} fusion(s32[15,32,128]{2,0,1:T(8,128)S(1)} %bitcast.115, bf16[1,2,15,32,128]{4,3,2,1,0:T(8,128)(2,1)S(1)} %constant_dynamic-slice_fusion.5), kind=kOutput, calls=%fused_computation.4.clone.1 | convolution fusion | flops 73728000 | bytes 552960 | tf_op jit(solution)/shard_map/while/body/eval_jaxpr/while/body/eval_jaxpr/skji,kjiq->sqj/dot_general | solution.py:53
  130.2 10.5 %fusion.53 = f32[1,2,240,32]{2,1,3,0:T(2,128)S(1)} fusion(s32[15,32,128]{2,0,1:T(8,128)S(1)} %bitcast.115, bf16[1,2,15,32,128]{4,3,2,1,0:T(8,128)(2,1)S(1)} %constant_dynamic-slice_fusion.5), kind=kOutput, calls=%fused_computation.4.clone.1 | convolution fusion | flops 73728000 | bytes 552960 | tf_op jit(solution)/shard_map/while/body/eval_jaxpr/while/body/eval_jaxpr/skji,kjiq->sqj/dot_general | solution.py:53
  143.4 10.5 %fusion.53 = f32[1,2,240,32]{2,1,3,0:T(2,128)S(1)} fusion(s32[15,32,128]{2,0,1:T(8,128)S(1)} %bitcast.115, bf16[1,2,15,32,128]{4,3,2,1,0:T(8,128)(2,1)S(1)} %constant_dynamic-slice_fusion.5), kind=kOutput, calls=%fused_computation.4.clone.1 | convolution fusion | flops 73728000 | bytes 552960 | tf_op jit(solution)/shard_map/while/body/eval_jaxpr/while/body/eval_jaxpr/skji,kjiq->sqj/dot_general | solution.py:53
  156.6 10.5 %fusion.53 = f32[1,2,240,32]{2,1,3,0:T(2,128)S(1)} fusion(s32[15,32,128]{2,0,1:T(8,128)S(1)} %bitcast.115, bf16[1,2,15,32,128]{4,3,2,1,0:T(8,128)(2,1)S(1)} %constant_dynamic-slice_fusion.5), kind=kOutput, calls=%fused_computation.4.clone.1 | convolution fusion | flops 73728000 | bytes 552960 | tf_op jit(solution)/shard_map/while/body/eval_jaxpr/while/body/eval_jaxpr/skji,kjiq->sqj/dot_general | solution.py:53
  169.8 10.5 %fusion.53 = f32[1,2,240,32]{2,1,3,0:T(2,128)S(1)} fusion(s32[15,32,128]{2,0,1:T(8,128)S(1)} %bitcast.115, bf16[1,2,15,32,128]{4,3,2,1,0:T(8,128)(2,1)S(1)} %constant_dynamic-slice_fusion.5), kind=kOutput, calls=%fused_computation.4.clone.1 | convolution fusion | flops 73728000 | bytes 552960 | tf_op jit(solution)/shard_map/while/body/eval_jaxpr/while/body/eval_jaxpr/skji,kjiq->sqj/dot_general | solution.py:53
  183.0 10.5 %fusion.53 = f32[1,2,240,32]{2,1,3,0:T(2,128)S(1)} fusion(s32[15,32,128]{2,0,1:T(8,128)S(1)} %bitcast.115, bf16[1,2,15,32,128]{4,3,2,1,0:T(8,128)(2,1)S(1)} %constant_dynamic-slice_fusion.5), kind=kOutput, calls=%fused_computation.4.clone.1 | convolution fusion | flops 73728000 | bytes 552960 | tf_op jit(solution)/shard_map/while/body/eval_jaxpr/while/body/eval_jaxpr/skji,kjiq->sqj/dot_general | solution.py:53
  196.2 10.5 %fusion.53 = f32[1,2,240,32]{2,1,3,0:T(2,128)S(1)} fusion(s32[15,32,128]{2,0,1:T(8,128)S(1)} %bitcast.115, bf16[1,2,15,32,128]{4,3,2,1,0:T(8,128)(2,1)S(1)} %constant_dynamic-slice_fusion.5), kind=kOutput, calls=%fused_computation.4.clone.1 | convolution fusion | flops 73728000 | bytes 552960 | tf_op jit(solution)/shard_map/while/body/eval_jaxpr/while/body/eval_jaxpr/skji,kjiq->sqj/dot_general | solution.py:53
  209.4 10.5 %fusion.53 = f32[1,2,240,32]{2,1,3,0:T(2,128)S(1)} fusion(s32[15,32,128]{2,0,1:T(8,128)S(1)} %bitcast.115, bf16[1,2,15,32,128]{4,3,2,1,0:T(8,128)(2,1)S(1)} %constant_dynamic-slice_fusion.5), kind=kOutput, calls=%fused_computation.4.clone.1 | convolution fusion | flops 73728000 | bytes 552960 | tf_op jit(solution)/shard_map/while/body/eval_jaxpr/while/body/eval_jaxpr/skji,kjiq->sqj/dot_general | solution.py:53
  222.6 10.5 %fusion.53 = f32[1,2,240,32]{2,1,3,0:T(2,128)S(1)} fusion(s32[15,32,128]{2,0,1:T(8,128)S(1)} %bitcast.115, bf16[1,2,15,32,128]{4,3,2,1,0:T(8,128)(2,1)S(1)} %constant_dynamic-slice_fusion.5), kind=kOutput, calls=%fused_computation.4.clone.1 | convolution fusion | flops 73728000 | bytes 552960 | tf_op jit(solution)/shard_map/while/body/eval_jaxpr/while/body/eval_jaxpr/skji,kjiq->sqj/dot_general | solution.py:53
  235.8 10.5 %fusion.53 = f32[1,2,240,32]{2,1,3,0:T(2,128)S(1)} fusion(s32[15,32,128]{2,0,1:T(8,128)S(1)} %bitcast.115, bf16[1,2,15,32,128]{4,3,2,1,0:T(8,128)(2,1)S(1)} %constant_dynamic-slice_fusion.5), kind=kOutput, calls=%fused_computation.4.clone.1 | convolution fusion | flops 73728000 | bytes 552960 | tf_op jit(solution)/shard_map/while/body/eval_jaxpr/while/body/eval_jaxpr/skji,kjiq->sqj/dot_general | solution.py:53
  249.0 10.5 %fusion.53 = f32[1,2,240,32]{2,1,3,0:T(2,128)S(1)} fusion(s32[15,32,128]{2,0,1:T(8,128)S(1)} %bitcast.115, bf16[1,2,15,32,128]{4,3,2,1,0:T(8,128)(2,1)S(1)} %constant_dynamic-slice_fusion.5), kind=kOutput, calls=%fused_computation.4.clone.1 | convolution fusion | flops 73728000 | bytes 552960 | tf_op jit(solution)/shard_map/while/body/eval_jaxpr/while/body/eval_jaxpr/skji,kjiq->sqj/dot_general | solution.py:53
  262.2 10.5 %fusion.53 = f32[1,2,240,32]{2,1,3,0:T(2,128)S(1)} fusion(s32[15,32,128]{2,0,1:T(8,128)S(1)} %bitcast.115, bf16[1,2,15,32,128]{4,3,2,1,0:T(8,128)(2,1)S(1)} %constant_dynamic-slice_fusion.5), kind=kOutput, calls=%fused_computation.4.clone.1 | convolution fusion | flops 73728000 | bytes 552960 | tf_op jit(solution)/shard_map/while/body/eval_jaxpr/while/body/eval_jaxpr/skji,kjiq->sqj/dot_general | solution.py:53
  275.4 10.5 %fusion.53 = f32[1,2,240,32]{2,1,3,0:T(2,128)S(1)} fusion(s32[15,32,128]{2,0,1:T(8,128)S(1)} %bitcast.115, bf16[1,2,15,32,128]{4,3,2,1,0:T(8,128)(2,1)S(1)} %constant_dynamic-slice_fusion.5), kind=kOutput, calls=%fused_computation.4.clone.1 | convolution fusion | flops 73728000 | bytes 552960 | tf_op jit(solution)/shard_map/while/body/eval_jaxpr/while/body/eval_jaxpr/skji,kjiq->sqj/dot_general | solution.py:53
  288.6 10.5 %fusion.53 = f32[1,2,240,32]{2,1,3,0:T(2,128)S(1)} fusion(s32[15,32,128]{2,0,1:T(8,128)S(1)} %bitcast.115, bf16[1,2,15,32,128]{4,3,2,1,0:T(8,128)(2,1)S(1)} %constant_dynamic-slice_fusion.5), kind=kOutput, calls=%fused_computation.4.clone.1 | convolution fusion | flops 73728000 | bytes 552960 | tf_op jit(solution)/shard_map/while/body/eval_jaxpr/while/body/eval_jaxpr/skji,kjiq->sqj/dot_general | solution.py:53
  299.7 2.9 reshape.181
  307.6 13.5 %all-gather.3 = f32[4,4,75]{2,1,0:T(4,128)S(1)} all-gather(f32[1,4,75]{2,1,0:T(4,128)S(1)} %bitcast.129), channel_id=3, replica_groups=mesh['lon'=4,'lat'=4,'mem'=2] {'lat'}, dimensions={0}, use_global_device_ids=true | all-gather | bytes 6000 | tf_op jit(solution)/shard_map/all_gather | solution.py:18
  321.2 10.6 %reduce-scatter.9.cloned.1.call-done = f32[1,1,3,2,80,32]{4,5,3,2,0,1:T(8,128)} async-done(((f32[1,4,3,2,80,32]{4,5,3,2,0,1:T(8,128)}), f32[1,1,3,2,80,32]{4,5,3,2,0,1:T(8,128)}) %reduce-scatter.9.cloned.1.call-update) | async-done | bytes 61456
  334.5 12.0 %all-gather.2 = f32[4,4,80]{2,1,0:T(4,128)S(1)} all-gather(f32[1,4,80]{2,1,0:T(4,128)S(1)} %bitcast.130), channel_id=2, replica_groups=mesh['lon'=4,'lat'=4,'mem'=2] {'lat'}, dimensions={0}, use_global_device_ids=true | all-gather | bytes 6400 | tf_op jit(solution)/shard_map/all_gather | solution.py:18
  349.5 16.8 %all-reduce.9.cloned.1.call-done = (f32[1,4,2,75,32]{3,4,2,1,0:T(8,128)}, f32[1,4,2,80,32]{3,4,2,1,0:T(8,128)}) async-done(((f32[1,4,2,75,32]{3,4,2,1,0:T(8,128)}, f32[1,4,2,80,32]{3,4,2,1,0:T(8,128)}), (f32[1,4,2,75,32]{3,4,2,1,0:T(8,128)}, f32[1,4,2,80,32]{3,4,2,1,0:T(8,128)})) %all-reduce.9.cloned.1.call-update) | async-done | bytes 158736 | tf_op jit(solution)/shard_map/psum | solution.py:131
  369.7 19.7 %all-reduce.7.cloned.1.call-done = (f32[1,4,2,75,32]{3,4,2,1,0:T(8,128)}, f32[1,4,2,80,32]{3,4,2,1,0:T(8,128)}) async-done(((f32[1,4,2,75,32]{3,4,2,1,0:T(8,128)}, f32[1,4,2,80,32]{3,4,2,1,0:T(8,128)}), (f32[1,4,2,75,32]{3,4,2,1,0:T(8,128)}, f32[1,4,2,80,32]{3,4,2,1,0:T(8,128)})) %all-reduce.7.cloned.1.call-update) | async-done | bytes 158736 | tf_op jit(solution)/shard_map/psum | solution.py:134
  (164 shorter events, 84.1 us)
Async XLA Ops:
  7.2 297.2 %reduce-scatter.7.cloned.1.call-start = ((), (), s32[]{:S(2)}) async-start(), calls=%async_computation.2 | async-start | bytes 491520
  7.2 1.7 copy-start.6
  8.9 3.3 copy-start.3
  9.0 5.1 %copy-start.1 = (f32[75,32,128]{2,1,0:T(8,128)}, f32[75,32,128]{2,1,0:T(8,128)S(1)}, u32[]{:S(2)}) copy-start(f32[75,32,128]{2,1,0:T(8,128)S(1)} %compare_convert_fusion) | copy-start | bytes 3686404
  9.1 3.1 copy-start.7
  12.2 1.9 copy-start.4
  17.8 314.0 %reduce-scatter.9.cloned.1.call-start = ((), (), s32[]{:S(2)}) async-start(), calls=%async_computation.3 | async-start | bytes 491520
  18.0 2.9 copy-start.2
  18.0 3.2 copy-start.5
  23.4 2.3 copy-start
  304.3 62.1 %all-reduce.9.cloned.1.call-start = ((), (), s32[]{:S(2)}) async-start(), calls=%async_computation.5 | async-start | bytes 524288 | tf_op jit(solution)/shard_map/psum | solution.py:131
  349.3 40.0 %all-reduce.7.cloned.1.call-start = ((), (), s32[]{:S(2)}) async-start(), calls=%async_computation.4 | async-start | bytes 524288 | tf_op jit(solution)/shard_map/psum | solution.py:134
Sparse Core Ops, SparseCore 0:
  17.9 27.4 reduce-scatter.6
  304.4 27.3 reduce-scatter.8
  349.4 16.9 all-reduce.8
  369.8 19.4 all-reduce.6
where the time goes:
time: 401 us; the launch traced here: 399 us
  matrix products  213 us (53%)
  local copies, waits for them, and re-layouts  63.7 us (16%)
  waiting for transfers between devices  47.2 us (12%)
  other arithmetic  34.8 us (9%)
  blocking collectives  25.5 us (6%)
  between operations  14 us (3%)
    dot_general x20, matrix products, one_block(): jnp.einsum('skji,kjiq->sqj', packed[0], onehot, preferred_element_type=jn...  209 us
    dynamic_slice x60, local copies, waits for them, and re-layouts, class_sums(): per_block = lax.map(one_block, (weighted, combined))  41.5 us
    all_gather x2, blocking collectives, carried_in(): everything = jax.tree.map(lambda part: lax.all_gather(part, axis), shard)  25.5 us
    psum x1, waiting for transfers between devices, body(): lax.psum((jnp.sum(jnp.square(class_moc - class_mean), 0), jnp.sum(jnp.squ...  19.7 us
    psum x1, waiting for transfers between devices, body(): lax.psum((jnp.sum(class_moc, 0), jnp.sum(depth_moc, 0)), 'mem')  16.8 us
    dynamic_update_slice x20, local copies, waits for them, and re-layouts, class_sums(): per_block = lax.map(one_block, (weighted, combined))  12.8 us
    unnamed x6, waiting for transfers between devices  10.7 us
  transfers between devices with their start and end apart: 4, of which 3 were waited for; matrix products, arithmetic and copies ran while one was open for 72% of the time, Pallas kernels for 0%

commit v1 on v0

v1 whole, which is shorter than its diff:
```python
import math

import jax
import jax.numpy as jnp
from jax import lax
from jax.experimental import pallas as pl
from jax.experimental.pallas import tpu as pltpu
from jax.sharding import PartitionSpec as P

CLASSES = 80
BASINS = 3
REGIONS = BASINS + 1
LOW = 32
SUB = 8


north_unit = 0.02
up_unit = 0.01

F32, BF16 = jnp.float32, jnp.bfloat16
NT = (((1,), (1,)), ((), ()))
NN = (((1,), (0,)), ((), ()))


def round_up(n, k):
    return -(-n // k) * k


def iota(shape, axis):
    return lax.broadcasted_iota(jnp.int32, shape, axis)


def split(x):
    high = x.astype(BF16)
    return high, (x - high.astype(F32)).astype(BF16)


def exact_dot(ones, x, dims, ones_first=True):
    high, low = split(x)
    if ones_first:
        return lax.dot_general(ones, high, dims, preferred_element_type=F32) + lax.dot_general(
            ones, low, dims, preferred_element_type=F32
        )
    return lax.dot_general(high, ones, dims, preferred_element_type=F32) + lax.dot_general(
        low, ones, dims, preferred_element_type=F32
    )


def sizes_of(levels, rows):
    highs = round_up(-(-BASINS * CLASSES // LOW), 2)
    return dict(
        levels=levels,
        rows=rows,
        highs=highs,
        deep=round_up(levels, 16),
        lanes=REGIONS * rows,
        block=max(c for c in range(1, 8) if levels % c == 0),
    )


def prepare(sz, basin, consts):
    base_ref, mask_ref, upto_class, upto_level, upto_row = consts
    rows, lanes = sz["rows"], sz["lanes"]
    base_ref[...] = jnp.where(basin > 0, (basin - 1) * CLASSES, -LOW * 64)
    regions = [basin > 0] + [basin == r for r in range(1, REGIONS)]
    mask_ref[...] = jnp.concatenate(
        [jnp.where(r, 1.0, 0.0) for r in regions], axis=0
    ).astype(BF16)
    shape = upto_class.shape
    q = iota(shape, 1) // SUB
    cls = jnp.where(q < CLASSES, q, jnp.where(q < 2 * CLASSES, q - CLASSES, q - 2 * CLASSES))
    upto_class[...] = jnp.where(cls <= iota(shape, 0), 1.0, 0.0).astype(BF16)
    shape = upto_level.shape
    upto_level[...] = jnp.where(iota(shape, 1) <= iota(shape, 0), 1.0, 0.0).astype(BF16)
    shape = upto_row.shape
    a, b = iota(shape, 0), iota(shape, 1)
    upto_row[...] = jnp.where((a // rows == b // rows) & (a <= b), 1.0, 0.0).astype(BF16)


def month_tables(sz, north, up, dens, thick, coef, consts, work, put):
    base_ref, mask_ref, upto_class, upto_level, upto_row = consts
    acc, flux, depth = work
    rows, highs, levels, lanes = sz["rows"], sz["highs"], sz["levels"], sz["lanes"]
    block = sz["block"]
    acc[...] = jnp.zeros_like(acc)
    one, zero = jnp.ones((2 * SUB, 128), BF16), jnp.zeros((2 * SUB, 128), BF16)

    def step(t, carry):
        for pair in range(rows // (2 * SUB)):
            cells = slice(pair * 2 * SUB, (pair + 1) * 2 * SUB)
            lhs, rhs = ([], []), ([], [])
            for kk in range(block):
                k = t * block + kk
                depth_k = thick[k, cells, :]
                nf = north[k, cells, :].astype(F32) * coef[0, cells, :] * (
                    depth_k.astype(F32) * 0.001
                )
                rf = up[k, cells, :].astype(F32) * jnp.where(depth_k > 0, coef[1, cells, :], 0.0)
                flux[0, k, cells, :] = nf.astype(BF16)
                flux[1, k, cells, :] = rf.astype(BF16)
                q = base_ref[cells, :] + dens[k, cells, :]
                hi, lo = (q >> 5).astype(F32), (q & (LOW - 1)).astype(F32)
                for half in range(2):
                    part = slice(half * SUB, (half + 1) * SUB)
                    twin = lambda x, d: jnp.concatenate([x[part], x[part] - d], 0).astype(BF16)
                    both = lambda x: jnp.concatenate([x[part], x[part]], 0).astype(BF16)
                    hp, lp, nd, rd = twin(hi, 1.0), twin(lo, 1.0), both(nf), both(rf)
                    rhs[half].append(
                        jnp.concatenate(
                            [jnp.where(lp == BF16(2 * p), one, zero) for p in range(LOW // 2)], 0
                        )
                    )
                    hits = [hp == BF16(2 * p) for p in range(highs // 2)]
                    lhs[half].append(
                        jnp.concatenate(
                            [jnp.where(h, nd, zero) for h in hits]
                            + [jnp.where(h, rd, zero) for h in hits],
                            0,
                        )
                    )
            for half in range(2):
                acc[2 * pair + half] += lax.dot_general(
                    jnp.concatenate(lhs[half], 1),
                    jnp.concatenate(rhs[half], 1),
                    NT,
                    preferred_element_type=F32,
                )
        return carry

    lax.fori_loop(0, levels // block, step, 0)

    own = iota((SUB, LOW * SUB), 0) == iota((SUB, LOW * SUB), 1) % SUB
    q = iota((rows, highs * LOW * SUB), 1) // SUB
    row_own = iota((rows, lanes), 0) == iota((rows, lanes), 1) % rows
    for s in range(2):
        grid = jnp.concatenate(
            [
                jnp.concatenate(
                    [
                        jnp.where(own, acc[g, pl.ds((s * highs + h) * SUB, SUB), :], 0.0)
                        for h in range(highs)
                    ],
                    1,
                )
                for g in range(rows // SUB)
            ],
            0,
        )
        total = None
        for piece in split(grid):
            piece = piece.astype(F32)
            parts = [piece] + [
                jnp.where((q >= b * CLASSES) & (q < (b + 1) * CLASSES), piece, 0.0)
                for b in range(BASINS)
            ]
            term = lax.dot_general(
                upto_class[...],
                jnp.concatenate(parts, 0).astype(BF16),
                NT,
                preferred_element_type=F32,
            )
            total = term if total is None else total + term
        found = lax.dot_general(
            flux[s].reshape(levels * rows, 128), mask_ref[...], NT, preferred_element_type=F32
        )
        found = jnp.where(row_own[None], found.reshape(levels, rows, lanes), 0.0)
        depth[0:levels, :] = jnp.sum(found, axis=1)
        if s == 0:
            put(0, total)
            put(2, exact_dot(upto_level[...], depth[...], NN))
        else:
            put(1, exact_dot(upto_row[...], total, NN, False))
            put(3, exact_dot(upto_row[...], depth[...], NN, False))


def table_rows(sz):
    return [0, CLASSES, 2 * CLASSES, 2 * CLASSES + sz["deep"], 2 * (CLASSES + sz["deep"])]


def const_shapes(sz, lons):
    rows, lanes = sz["rows"], sz["lanes"]
    return [
        pltpu.VMEM((rows, lons), jnp.int32),
        pltpu.VMEM((lanes, lons), BF16),
        pltpu.VMEM((CLASSES, sz["highs"] * LOW * SUB), BF16),
        pltpu.VMEM((sz["deep"], sz["deep"]), BF16),
        pltpu.VMEM((lanes, lanes), BF16),
    ]


def work_shapes(sz, lons):
    rows = sz["rows"]
    return [
        pltpu.VMEM((rows // SUB, 2 * sz["highs"] * SUB, LOW * SUB), F32),
        pltpu.VMEM((2, sz["levels"], rows, lons), BF16),
        pltpu.VMEM((sz["deep"], sz["lanes"]), F32),
    ]


def local_tables(sz, north_vel, up_vel, dens_class, thickness, basin_id, coef):
    months, levels, rows, lons = north_vel.shape
    at = table_rows(sz)

    def kernel(north, up, dens, thick, basin, coef, out, *scratch):
        consts, work = scratch[:5], scratch[5:]

        @pl.when(pl.program_id(0) == 0)
        def _():
            prepare(sz, basin[...], consts)
            work[2][...] = jnp.zeros_like(work[2])

        def put(i, x):
            out[0, at[i] : at[i + 1], :] = x

        month_tables(
            sz, north.at[0], up.at[0], dens.at[0], thick, coef, consts, work, put
        )

    month = pl.BlockSpec((1, levels, rows, lons), lambda m: (m, 0, 0, 0))
    whole = lambda a: pl.BlockSpec(a.shape, lambda m: (0,) * a.ndim)
    return pl.pallas_call(
        kernel,
        grid=(months,),
        out_shape=jax.ShapeDtypeStruct((months, at[-1], sz["lanes"]), F32),
        in_specs=[month, month, month, whole(thickness), whole(basin_id), whole(coef)],
        out_specs=pl.BlockSpec((1, at[-1], sz["lanes"]), lambda m: (m, 0, 0)),
        scratch_shapes=const_shapes(sz, lons) + work_shapes(sz, lons),
        compiler_params=pltpu.CompilerParams(
            dimension_semantics=("arbitrary",), vmem_limit_bytes=60 * 2**20
        ),
    )(north_vel, up_vel, dens_class, thickness, basin_id, coef)


def coefficients(rows, lons):
    first = lax.axis_index("lat") * rows
    total = rows * lax.axis_size("lat")
    row_index = first + jnp.arange(rows, dtype=jnp.int32)
    latitude = (-78.0 + 156.0 * (row_index.astype(F32) + 0.5) / total) * (math.pi / 180.0)
    width = jnp.cos(latitude)
    coef = jnp.stack([north_unit * width, up_unit * width])
    return jnp.broadcast_to(coef[:, :, None], (2, rows, lons))


def body(north_vel, up_vel, dens_class, thickness, basin_id):
    _, months, levels, rows, lons = north_vel.shape
    sz = sizes_of(levels, rows)
    at = table_rows(sz)
    table = local_tables(
        sz, north_vel[0], up_vel[0], dens_class[0], thickness, basin_id, coefficients(rows, lons)
    )
    table = lax.psum_scatter(table, "lon", scatter_dimension=0, tiled=True)
    own, lanes = table.shape[0], table.shape[-1]
    split_up = lambda i, n: jnp.moveaxis(
        table[:, at[i] : at[i] + n].reshape(own, n, REGIONS, rows), 2, 1
    )
    cn, cr = split_up(0, CLASSES), split_up(1, CLASSES)
    dn, dr = split_up(2, levels), split_up(3, levels)
    ends = lax.all_gather(jnp.concatenate([cr[..., -1], dr[..., -1]], 2), "lat")
    south = jnp.arange(ends.shape[0]) < lax.axis_index("lat")
    carry = jnp.sum(jnp.where(south[:, None, None, None], ends, 0.0), 0)
    cr = cr + carry[:, :, :CLASSES, None]
    dr = dr + carry[:, :, CLASSES:, None]
    moc = jnp.concatenate([jnp.stack([cn, cr], 2), jnp.stack([dn, dr], 2)], 3)
    members = lax.axis_size("mem")
    mean = lax.psum(moc, "mem") / members
    spread = jnp.sqrt(lax.psum(jnp.square(moc - mean), "mem") / (members - 1))
    return (
        mean[..., CLASSES:, :],
        spread[..., CLASSES:, :],
        mean[..., :CLASSES, :],
        spread[..., :CLASSES, :],
    )


def solution(mesh):
    in_specs = (
        P("mem", None, None, "lat", "lon"),
        P("mem", None, None, "lat", "lon"),
        P("mem", None, None, "lat", "lon"),
        P(None, "lat", "lon"),
        P("lat", "lon"),
    )
    out_specs = (P("lon", None, None, None, "lat"),) * 4
    return jax.shard_map(body, mesh=mesh, in_specs=in_specs, out_specs=out_specs, check_vma=False)
```

time: 401 us -> 168 us (0.42)
  matrix products: 213 us -> 0 us
  local copies, waits for them, and re-layouts: 63.7 us -> 8.61 us
  Pallas kernels: 0 us -> 42.9 us
  waiting for transfers between devices: 47.2 us -> 85.9 us
  other arithmetic: 34.8 us -> 2.88 us
  blocking collectives: 25.5 us -> 13.2 us
    dot_general x22 -> x0, matrix products: 213 us -> none  [the longest x20 209 us: one_block(): jnp.einsum('skji,kjiq->sqj', packed[0], onehot, preferred_element_type=jn...]
    pallas_call x0 -> x1, Pallas kernels: none -> 42.9 us  [local_tables(): pl.pallas_call(kernel, grid=(months,), out_shape=jax.ShapeDtypeStruct((mo...]
    dynamic_slice x60 -> x0, local copies, waits for them, and re-layouts: 41.5 us -> none  [class_sums(): per_block = lax.map(one_block, (weighted, combined))]
    unnamed x6 -> x4, waiting for transfers between devices: 10.7 us -> 49 us
    dynamic_update_slice x20 -> x0, local copies, waits for them, and re-layouts: 12.8 us -> none  [class_sums(): per_block = lax.map(one_block, (weighted, combined))]
    all_gather x2 -> x1, blocking collectives: 25.5 us -> 13.2 us  [body(): ends = lax.all_gather(jnp.concatenate([cr[..., -1], dr[..., -1]], 2), 'lat')]
    convert_element_type x5 -> x0, other arithmetic: 8.95 us -> none  [the longest x2 5.95 us: local_tables(): north_flux = (north_vel.astype(jnp.float32) * (north_unit * zonal_width)[...]
    unnamed x6 -> x0, other arithmetic: 5.78 us -> none
  transfers between devices with their start and end apart: 4 -> 3, of which waited for: 3 -> 3; matrix products, arithmetic and copies ran while one was open for 72% -> 1% of each run, Pallas kernels for 0% -> 0%
where the time goes in v1:
time: 168 us; the launch traced here: 167 us
  waiting for transfers between devices  85.9 us (51%)
  Pallas kernels  42.9 us (26%)
  between operations  13.9 us (8%)
  blocking collectives  13.2 us (8%)
  local copies, waits for them, and re-layouts  8.61 us (5%)
  other arithmetic  2.88 us (2%)
    unnamed x4, waiting for transfers between devices  49 us
    pallas_call x1, Pallas kernels, local_tables(): pl.pallas_call(kernel, grid=(months,), out_shape=jax.ShapeDtypeStruct((mo...  42.9 us
    psum x1, waiting for transfers between devices, body(): spread = jnp.sqrt(lax.psum(jnp.square(moc - mean), 'mem') / (members - 1))  18.5 us
    psum x1, waiting for transfers between devices, body(): mean = lax.psum(moc, 'mem') / members  18.3 us
    all_gather x1, blocking collectives, body(): ends = lax.all_gather(jnp.concatenate([cr[..., -1], dr[..., -1]], 2), 'lat')  13.2 us
    unnamed x11, local copies, waits for them, and re-layouts  3.62 us
  transfers between devices with their start and end apart: 3, of which 3 were waited for; matrix products, arithmetic and copies ran while one was open for 1% of the time, Pallas kernels for 0%

profile of v1, /device:TPU:0, one launch (start us, length us, event | category | flops | bytes accessed | tf_op | source)
XLA Modules:
  0.0 167.5 jit_solution(14457517982100808339)
XLA Ops:
  7.2 0.0 all-reduce.9.cloned.1.call-start
  7.3 0.7 broadcast_in_dim.14.coef
  8.0 42.9 %shard_map.84 = f32[4,320,128]{2,1,0:T(8,128)} custom-call(bf16[4,75,32,128]{3,2,1,0:T(8,128)(2,1)} %bitcast.36, bf16[4,75,32,128]{3,2,1,0:T(8,128)(2,1)} %bitcast.37, s32[4,75,32,128]{3,2,1,0:T(8,128)} %bitcast.35, s32[75,32,128]{2,1,0:T(8,128)} %thick.1, s32[32,128]{1,0:T(8,128)} %basin.1, f32[2,32,128]{2,1,0:T(8,128)} %broadcast_in_dim.14.coef), custom_call_target="tpu_custom_call" | custom-call | tf_op jit(solution)/shard_map/pallas_call | solution.py:221
  50.9 0.0 all-reduce.9.cloned.1.call-update
  50.9 0.0 all-reduce.5.cloned.1.call-start
  51.0 0.0 copy-done
  51.0 0.6 dynamic-slice
  51.6 49.0 %all-reduce.9.cloned.1.call-done = f32[4,320,128]{2,1,0:T(8,128)} async-done(((f32[4,320,128]{2,1,0:T(8,128)}), f32[4,320,128]{2,1,0:T(8,128)}) %all-reduce.9.cloned.1.call-update) | async-done | bytes 655376
  100.6 1.5 constant_dynamic-slice_fusion.3
  102.1 0.1 copy.31
  102.2 1.5 constant_dynamic-slice_fusion.2
  103.7 0.1 copy.30
  103.8 0.1 pad_maximum_fusion
  103.9 13.2 %all-gather = f32[4,4,155]{2,1,0:T(4,128)S(1)} all-gather(f32[1,4,155]{2,1,0:T(4,128)S(1)} %pad_maximum_fusion), channel_id=2, replica_groups=mesh['lon'=4,'lat'=4,'mem'=2] {'lat'}, dimensions={0}, use_global_device_ids=true | all-gather | bytes 12400 | tf_op jit(solution)/shard_map/all_gather | solution.py:258
  117.1 0.1 fusion
  117.2 0.1 slice_bitcast_fusion
  117.3 0.1 copy.32
  117.4 0.1 copy.29
  117.5 0.9 maximum_maximum_fusion
  118.3 0.0 all-reduce.5.cloned.1.call-update
  118.4 0.0 all-reduce.7.cloned.1.call-start
  118.4 18.3 %all-reduce.5.cloned.1.call-done = f32[1,4,2,155,32]{3,4,1,2,0:T(8,128)} async-done(((f32[1,4,2,155,32]{3,4,1,2,0:T(8,128)}), f32[1,4,2,155,32]{3,4,1,2,0:T(8,128)}) %all-reduce.5.cloned.1.call-update) | async-done | bytes 158736 | tf_op jit(solution)/shard_map/psum | solution.py:265
  136.7 1.8 %subtract_multiply_fusion = (f32[1,4,2,155,32]{3,4,1,2,0:T(8,128)}, f32[1,4,2,155,32]{3,4,1,2,0:T(8,128)S(1)}) fusion(f32[1,4,2,155,32]{3,4,1,2,0:T(8,128)} %all-reduce.5.cloned.1.call-done, f32[1,4,1,75,32]{3,4,1,2,0:T(8,128)S(1)} %add_bitcast_fusion, f32[1,4,1,75,32]{3,4,1,2,0:T(8,128)S(1)} %bitcast.39, f32[1,4,1,80,32]{3,4,1,2,0:T(8,128)S(1)} %add_bitcast_fusion.1, ...), kind=kLoop, calls=%fused_computation.1 | loop fusion | flops 238080 | bytes 634880 | tf_op jit(solution)/shard_map/square | solution.py:266
  138.5 0.0 all-reduce.7.cloned.1.call-update
  138.5 0.1 slice.52
  138.6 0.7 copy.25
  139.3 0.7 copy.27
  140.0 18.5 %all-reduce.7.cloned.1.call-done = f32[1,4,2,155,32]{3,4,1,2,0:T(8,128)} async-done(((f32[1,4,2,155,32]{3,4,1,2,0:T(8,128)}), f32[1,4,2,155,32]{3,4,1,2,0:T(8,128)}) %all-reduce.7.cloned.1.call-update) | async-done | bytes 158736 | tf_op jit(solution)/shard_map/psum | solution.py:266
  158.5 1.0 sqrt.3
  159.5 0.1 slice.53
  159.6 0.7 copy.26
  160.3 0.7 copy.28
  (11 shorter events, 0.1 us)
Async XLA Ops:
  7.2 93.4 %all-reduce.9.cloned.1.call-start = ((), (), s32[]{:S(2)}) async-start(), calls=%async_computation.2 | async-start | bytes 1310720
  8.0 43.0 %copy-start = (u32[32]{0:T(128)S(1)}, u32[32]{0:T(128)}, u32[]{:S(2)}) copy-start(u32[32]{0:T(128)} %constant.34) | copy-start | bytes 388
  50.9 85.8 %all-reduce.5.cloned.1.call-start = ((), (), s32[]{:S(2)}) async-start(), calls=%async_computation | async-start | bytes 524288 | tf_op jit(solution)/shard_map/psum | solution.py:265
  118.4 40.1 %all-reduce.7.cloned.1.call-start = ((), (), s32[]{:S(2)}) async-start(), calls=%async_computation.1 | async-start | bytes 524288 | tf_op jit(solution)/shard_map/psum | solution.py:266
Sparse Core Ops, SparseCore 0:
  51.0 49.4 all-reduce.8
  118.5 18.1 all-reduce.4
  139.0 19.4 all-reduce.6

commit v2 on v1

--- a/solution.py
+++ b/solution.py
@@ -197,79 +197,215 @@
     ]
 
 
-def local_tables(sz, north_vel, up_vel, dens_class, thickness, basin_id, coef):
-    months, levels, rows, lons = north_vel.shape
+def fused(sz, north_vel, up_vel, dens_class, thickness, basin_id):
+    _, months, levels, rows, lons = north_vel.shape
+    lanes, deep = sz["lanes"], sz["deep"]
     at = table_rows(sz)
-
-    def kernel(north, up, dens, thick, basin, coef, out, *scratch):
-        consts, work = scratch[:5], scratch[5:]
-
-        @pl.when(pl.program_id(0) == 0)
-        def _():
-            prepare(sz, basin[...], consts)
-            work[2][...] = jnp.zeros_like(work[2])
-
-        def put(i, x):
-            out[0, at[i] : at[i + 1], :] = x
-
-        month_tables(
-            sz, north.at[0], up.at[0], dens.at[0], thick, coef, consts, work, put
+    tall = at[-1]
+    ends = CLASSES + deep
+    devices, lats, members = (lax.axis_size(a) for a in ("lon", "lat", "mem"))
+    assert months == devices
+    far = [(de, dl) for dl in range(1, lats) for de in range(members)]
+
+    def kernel(north_h, up_h, dens_h, thick_h, basin_h, o_dm, o_ds, o_cm, o_cs, *scratch):
+        consts, work, rest = scratch[:5], scratch[5:8], scratch[8:]
+        (north, up, dens, thick, basin, coef, tab, inbox, mine, membox, tail, tailbox, final) = rest[:13]
+        in_sem, fix_sem, send, recv, msend, mrecv, tsend, trecv = rest[13:]
+        me, lat, mem = (lax.axis_index(a) for a in ("lon", "lat", "mem"))
+
+        def inputs(t):
+            month = lax.rem(me + 1 + t, devices)
+            return [
+                pltpu.make_async_copy(h.at[0, month], v.at[t], in_sem.at[t, i])
+                for i, (h, v) in enumerate(((north_h, north), (up_h, up), (dens_h, dens)))
+            ]
+
+        fixed = [
+            pltpu.make_async_copy(basin_h, basin, fix_sem.at[0]),
+            pltpu.make_async_copy(thick_h, thick, fix_sem.at[1]),
+        ]
+        for copy in fixed + inputs(0):
+            copy.start()
+        for t in range(1, devices):
+            for copy in inputs(t):
+                copy.start()
+
+        barrier = pltpu.get_barrier_semaphore()
+        peers = [{"lon": lax.rem(me + d, devices)} for d in range(1, devices)]
+        peers += [
+            {"lat": lax.rem(lat + dl, lats), "mem": lax.rem(mem + de, members)}
+            for dl in range(lats)
+            for de in range(members)
+            if dl or de
+        ]
+        for peer in peers:
+            pl.semaphore_signal(
+                barrier, inc=1, device_id=peer, device_id_type=pl.DeviceIdType.MESH
+            )
+
+        index = lat * rows + iota((rows, lons), 0)
+        latitude = (-78.0 + 156.0 * (index.astype(F32) + 0.5) / (rows * lats)) * (math.pi / 180.0)
+        width = jnp.cos(latitude)
+        coef[0] = north_unit * width
+        coef[1] = up_unit * width
+        work[2][...] = jnp.zeros_like(work[2])
+        fixed[0].wait()
+        prepare(sz, basin[...], consts)
+        fixed[1].wait()
+
+        def table_copy(t):
+            return pltpu.make_async_remote_copy(
+                src_ref=tab.at[t],
+                dst_ref=inbox.at[t],
+                send_sem=send.at[t],
+                recv_sem=recv.at[t],
+                device_id={"lon": lax.rem(me + 1 + t, devices)},
+                device_id_type=pl.DeviceIdType.MESH,
+            )
+
+        def one_month(t, carry):
+            for copy in inputs(t):
+                copy.wait()
+
+            def put(i, x):
+                tab[t, at[i] : at[i + 1], :] = x
+
+            month_tables(
+                sz, north.at[t], up.at[t], dens.at[t], thick, coef, consts, work, put
+            )
+
+            @pl.when(t == 0)
+            def _():
+                pl.semaphore_wait(barrier, len(peers))
+
+            @pl.when(t < devices - 1)
+            def _():
+                table_copy(t).start()
+
+            return carry
+
+        lax.fori_loop(0, devices, one_month, 0)
+
+        total = tab[devices - 1]
+        for t in range(devices - 1):
+            table_copy(t).wait_recv()
+            total = total + inbox[t]
+        mine[...] = total
+        copies = [
+            pltpu.make_async_remote_copy(
+                src_ref=mine,
+                dst_ref=membox.at[de - 1],
+                send_sem=msend.at[de - 1],
+                recv_sem=mrecv.at[de - 1],
+                device_id={"mem": lax.rem(mem + de, members)},
+                device_id_type=pl.DeviceIdType.MESH,
+            )
+            for de in range(1, members)
+        ]
+        for copy in copies:
+            copy.start()
+
+        pick = (iota((2 * SUB, lanes), 1) == iota((2 * SUB, lanes), 0) * rows + rows - 1)
+        pick = jnp.where(pick, 1.0, 0.0).astype(BF16)
+        rise = jnp.concatenate([mine[at[1] : at[2], :], mine[at[3] : at[4], :]], 0)
+        high, low = split(rise)
+        tail[...] = lax.dot_general(pick, high, NT, preferred_element_type=F32) + lax.dot_general(
+            pick, low, NT, preferred_element_type=F32
         )
-
-    month = pl.BlockSpec((1, levels, rows, lons), lambda m: (m, 0, 0, 0))
-    whole = lambda a: pl.BlockSpec(a.shape, lambda m: (0,) * a.ndim)
+        tails = [
+            pltpu.make_async_remote_copy(
+                src_ref=tail,
+                dst_ref=tailbox.at[i],
+                send_sem=tsend.at[i],
+                recv_sem=trecv.at[i],
+                device_id={"lat": lax.rem(lat + dl, lats), "mem": lax.rem(mem + de, members)},
+                device_id_type=pl.DeviceIdType.MESH,
+            )
+            for i, (de, dl) in enumerate(far)
+        ]
+        for copy in tails:
+            copy.start()
+
+        wide = (iota((2 * SUB, lanes), 1) // rows) == iota((2 * SUB, lanes), 0)
+        wide = jnp.where(wide, 1.0, 0.0).astype(BF16)
+        for copy in tails:
+            copy.wait_recv()
+        for copy in copies:
+            copy.wait_recv()
+        for de in range(members):
+            whole = mine if de == 0 else membox.at[de - 1]
+            south = jnp.zeros((2 * SUB, ends), F32)
+            for i, (other, dl) in enumerate(far):
+                if other == de:
+                    south = south + jnp.where(lat >= dl, tailbox[i], 0.0)
+            high, low = split(south)
+            tn = (((0,), (0,)), ((), ()))
+            carry = lax.dot_general(
+                high, wide, tn, preferred_element_type=F32
+            ) + lax.dot_general(low, wide, tn, preferred_element_type=F32)
+            final[de, at[0] : at[1], :] = whole[at[0] : at[1], :]
+            final[de, at[1] : at[2], :] = whole[at[1] : at[2], :] + carry[:CLASSES]
+            final[de, at[2] : at[3], :] = whole[at[2] : at[3], :]
+            final[de, at[3] : at[4], :] = whole[at[3] : at[4], :] + carry[CLASSES:]
+
+        for s in range(2):
+            for i, count, o_mean, o_spread in ((s, CLASSES, o_cm, o_cs), (2 + s, levels, o_dm, o_ds)):
+                part = [final[de, at[i] : at[i + 1], :] for de in range(members)]
+                mean = sum(part[1:], part[0]) / members
+                square = [jnp.square(x - mean) for x in part]
+                spread = jnp.sqrt(sum(square[1:], square[0]) / (members - 1))
+                for r in range(REGIONS):
+                    o_mean[0, r, s] = mean[:count, r * rows : (r + 1) * rows]
+                    o_spread[0, r, s] = spread[:count, r * rows : (r + 1) * rows]
+
+        for t in range(devices - 1):
+            table_copy(t).wait_send()
+        for copy in copies + tails:
+            copy.wait_send()
+
+    out = lambda n: jax.ShapeDtypeStruct((1, REGIONS, 2, n, rows), F32)
+    slots = max(1, devices - 1)
+    dma = pltpu.SemaphoreType.DMA
     return pl.pallas_call(
         kernel,
-        grid=(months,),
-        out_shape=jax.ShapeDtypeStruct((months, at[-1], sz["lanes"]), F32),
-        in_specs=[month, month, month, whole(thickness), whole(basin_id), whole(coef)],
-        out_specs=pl.BlockSpec((1, at[-1], sz["lanes"]), lambda m: (m, 0, 0)),
-        scratch_shapes=const_shapes(sz, lons) + work_shapes(sz, lons),
+        out_shape=[out(levels), out(levels), out(CLASSES), out(CLASSES)],
+        in_specs=[pl.BlockSpec(memory_space=pl.ANY)] * 5,
+        out_specs=[pl.BlockSpec(memory_space=pltpu.VMEM)] * 4,
+        scratch_shapes=const_shapes(sz, lons)
+        + work_shapes(sz, lons)
+        + [
+            pltpu.VMEM((months, levels, rows, lons), north_vel.dtype),
+            pltpu.VMEM((months, levels, rows, lons), up_vel.dtype),
+            pltpu.VMEM((months, levels, rows, lons), dens_class.dtype),
+            pltpu.VMEM((levels, rows, lons), thickness.dtype),
+            pltpu.VMEM((rows, lons), basin_id.dtype),
+            pltpu.VMEM((2, rows, lons), F32),
+            pltpu.VMEM((devices, tall, lanes), F32),
+            pltpu.VMEM((slots, tall, lanes), F32),
+            pltpu.VMEM((tall, lanes), F32),
+            pltpu.VMEM((members - 1, tall, lanes), F32),
+            pltpu.VMEM((2 * SUB, ends), F32),
+            pltpu.VMEM((len(far), 2 * SUB, ends), F32),
+            pltpu.VMEM((members, tall, lanes), F32),
+            dma((devices, 3)),
+            dma((2,)),
+            dma((slots,)),
+            dma((slots,)),
+            dma((members - 1,)),
+            dma((members - 1,)),
+            dma((len(far),)),
+            dma((len(far),)),
+        ],
         compiler_params=pltpu.CompilerParams(
-            dimension_semantics=("arbitrary",), vmem_limit_bytes=60 * 2**20
+            collective_id=0, has_side_effects=True, vmem_limit_bytes=60 * 2**20
         ),
-    )(north_vel, up_vel, dens_class, thickness, basin_id, coef)
-
-
-def coefficients(rows, lons):
-    first = lax.axis_index("lat") * rows
-    total = rows * lax.axis_size("lat")
-    row_index = first + jnp.arange(rows, dtype=jnp.int32)
-    latitude = (-78.0 + 156.0 * (row_index.astype(F32) + 0.5) / total) * (math.pi / 180.0)
-    width = jnp.cos(latitude)
-    coef = jnp.stack([north_unit * width, up_unit * width])
-    return jnp.broadcast_to(coef[:, :, None], (2, rows, lons))
+    )(north_vel, up_vel, dens_class, thickness, basin_id)
 
 
 def body(north_vel, up_vel, dens_class, thickness, basin_id):
-    _, months, levels, rows, lons = north_vel.shape
+    levels, rows = north_vel.shape[2:4]
     sz = sizes_of(levels, rows)
-    at = table_rows(sz)
-    table = local_tables(
-        sz, north_vel[0], up_vel[0], dens_class[0], thickness, basin_id, coefficients(rows, lons)
-    )
-    table = lax.psum_scatter(table, "lon", scatter_dimension=0, tiled=True)
-    own, lanes = table.shape[0], table.shape[-1]
-    split_up = lambda i, n: jnp.moveaxis(
-        table[:, at[i] : at[i] + n].reshape(own, n, REGIONS, rows), 2, 1
-    )
-    cn, cr = split_up(0, CLASSES), split_up(1, CLASSES)
-    dn, dr = split_up(2, levels), split_up(3, levels)
-    ends = lax.all_gather(jnp.concatenate([cr[..., -1], dr[..., -1]], 2), "lat")
-    south = jnp.arange(ends.shape[0]) < lax.axis_index("lat")
-    carry = jnp.sum(jnp.where(south[:, None, None, None], ends, 0.0), 0)
-    cr = cr + carry[:, :, :CLASSES, None]
-    dr = dr + carry[:, :, CLASSES:, None]
-    moc = jnp.concatenate([jnp.stack([cn, cr], 2), jnp.stack([dn, dr], 2)], 3)
-    members = lax.axis_size("mem")
-    mean = lax.psum(moc, "mem") / members
-    spread = jnp.sqrt(lax.psum(jnp.square(moc - mean), "mem") / (members - 1))
-    return (
-        mean[..., CLASSES:, :],
-        spread[..., CLASSES:, :],
-        mean[..., :CLASSES, :],
-        spread[..., :CLASSES, :],
-    )
+    return tuple(fused(sz, north_vel, up_vel, dens_class, thickness, basin_id))
 
 
 def solution(mesh):

time: 168 us -> 60.7 us (0.36)
  waiting for transfers between devices: 85.9 us -> 0 us
  between operations: 13.9 us -> 0.64 us
  blocking collectives: 13.2 us -> 0 us
  Pallas kernels: 42.9 us -> 52.7 us
  other arithmetic: 2.88 us -> 0 us
    unnamed x4 -> x0, waiting for transfers between devices: 49 us -> none
    psum x2 -> x0, waiting for transfers between devices: 36.8 us -> none  [the longest x1 18.5 us: body(): spread = jnp.sqrt(lax.psum(jnp.square(moc - mean), 'mem') / (members - 1))]
    all_gather x1 -> x0, blocking collectives: 13.2 us -> none  [body(): ends = lax.all_gather(jnp.concatenate([cr[..., -1], dr[..., -1]], 2), 'lat')]
    pallas_call x1, Pallas kernels: 42.9 us -> 52.7 us  [fused(): pl.pallas_call(kernel, out_shape=[out(levels), out(levels), out(CLASSES),...]
    pallas_call x0 -> x4, local copies, waits for them, and re-layouts: none -> 7.08 us  [fused(): pl.pallas_call(kernel, out_shape=[out(levels), out(levels), out(CLASSES),...]
    unnamed x11 -> x0, local copies, waits for them, and re-layouts: 3.62 us -> none
    slice x8 -> x0, local copies, waits for them, and re-layouts: 3.2 us -> none  [the longest x2 2.98 us: body(): table[:, at[i]:at[i] + n].reshape(own, n, REGIONS, rows)]
    square x1 -> x0, other arithmetic: 1.8 us -> none  [body(): spread = jnp.sqrt(lax.psum(jnp.square(moc - mean), 'mem') / (members - 1))]
  transfers between devices with their start and end apart: 3 -> 0, of which waited for: 3 -> 0; matrix products, arithmetic and copies ran while one was open for 1% -> 0% of each run, Pallas kernels for 0% -> 0%
where the time goes in v2:
time: 60.7 us; the launch traced here: 60.4 us
  Pallas kernels  52.7 us (87%)
  local copies, waits for them, and re-layouts  7.08 us (12%)
  between operations  0.64 us (1%)
    pallas_call x1, Pallas kernels, fused(): pl.pallas_call(kernel, out_shape=[out(levels), out(levels), out(CLASSES),...  52.7 us
    pallas_call x4, local copies, waits for them, and re-layouts, fused(): pl.pallas_call(kernel, out_shape=[out(levels), out(levels), out(CLASSES),...  7.08 us

profile of v2, /device:TPU:0, one launch (start us, length us, event | category | flops | bytes accessed | tf_op | source)
XLA Modules:
  0.0 60.4 jit_solution(4840363624687190340)
XLA Ops:
  0.6 52.7 %shard_map.84 = (f32[1,4,2,75,32]{4,3,2,1,0:T(8,128)}, f32[1,4,2,75,32]{4,3,2,1,0:T(8,128)}, f32[1,4,2,80,32]{4,3,2,1,0:T(8,128)}, f32[1,4,2,80,32]{4,3,2,1,0:T(8,128)}) custom-call(bf16[1,4,75,32,128]{4,3,2,1,0:T(8,128)(2,1)} %north_h.1, bf16[1,4,75,32,128]{4,3,2,1,0:T(8,128)(2,1)} %up_h.1, s32[1,4,75,32,128]{4,3,2,1,0:T(8,128)} %dens_h.1, ...), custom_call_target="tpu_custom_call" | custom-call | tf_op jit(solution)/shard_map/pallas_call | solution.py:369
  53.3 1.8 %copy.9 = f32[1,4,2,75,32]{3,4,2,1,0:T(8,128)} copy(f32[1,4,2,75,32]{4,3,2,1,0:T(8,128)} %get-tuple-element.4) | data formatting | bytes 153600 | tf_op jit(solution)/shard_map/pallas_call | solution.py:369
  55.1 1.8 %copy.10 = f32[1,4,2,75,32]{3,4,2,1,0:T(8,128)} copy(f32[1,4,2,75,32]{4,3,2,1,0:T(8,128)} %get-tuple-element.5) | data formatting | bytes 153600 | tf_op jit(solution)/shard_map/pallas_call | solution.py:369
  56.9 1.8 %copy.11 = f32[1,4,2,80,32]{3,4,2,1,0:T(8,128)} copy(f32[1,4,2,80,32]{4,3,2,1,0:T(8,128)} %get-tuple-element.6) | data formatting | bytes 163840 | tf_op jit(solution)/shard_map/pallas_call | solution.py:369
  58.6 1.8 %copy.12 = f32[1,4,2,80,32]{3,4,2,1,0:T(8,128)} copy(f32[1,4,2,80,32]{4,3,2,1,0:T(8,128)} %get-tuple-element.7) | data formatting | bytes 163840 | tf_op jit(solution)/shard_map/pallas_call | solution.py:369

commit v3 on v2

--- a/solution.py
+++ b/solution.py
@@ -10,7 +10,7 @@
 CLASSES = 80
 BASINS = 3
 REGIONS = BASINS + 1
-LOW = 32
+LOW = 16
 SUB = 8
 
 
@@ -54,7 +54,7 @@
         highs=highs,
         deep=round_up(levels, 16),
         lanes=REGIONS * rows,
-        block=max(c for c in range(1, 8) if levels % c == 0),
+        block=max(c for c in range(1, 32) if levels % c == 0),
     )
 
 
@@ -99,7 +99,7 @@
                 flux[0, k, cells, :] = nf.astype(BF16)
                 flux[1, k, cells, :] = rf.astype(BF16)
                 q = base_ref[cells, :] + dens[k, cells, :]
-                hi, lo = (q >> 5).astype(F32), (q & (LOW - 1)).astype(F32)
+                hi, lo = (q >> (LOW.bit_length() - 1)).astype(F32), (q & (LOW - 1)).astype(F32)
                 for half in range(2):
                     part = slice(half * SUB, (half + 1) * SUB)
                     twin = lambda x, d: jnp.concatenate([x[part], x[part] - d], 0).astype(BF16)
@@ -207,10 +207,10 @@
     assert months == devices
     far = [(de, dl) for dl in range(1, lats) for de in range(members)]
 
-    def kernel(north_h, up_h, dens_h, thick_h, basin_h, o_dm, o_ds, o_cm, o_cs, *scratch):
+    def kernel(north_h, up_h, dens_h, thick_h, basin_h, final, *scratch):
         consts, work, rest = scratch[:5], scratch[5:8], scratch[8:]
-        (north, up, dens, thick, basin, coef, tab, inbox, mine, membox, tail, tailbox, final) = rest[:13]
-        in_sem, fix_sem, send, recv, msend, mrecv, tsend, trecv = rest[13:]
+        (north, up, dens, thick, basin, coef, tab, inbox, mine, membox, tail, tailbox) = rest[:12]
+        in_sem, fix_sem, send, recv, msend, mrecv, tsend, trecv = rest[12:]
         me, lat, mem = (lax.axis_index(a) for a in ("lon", "lat", "mem"))
 
         def inputs(t):
@@ -348,29 +348,18 @@
             final[de, at[2] : at[3], :] = whole[at[2] : at[3], :]
             final[de, at[3] : at[4], :] = whole[at[3] : at[4], :] + carry[CLASSES:]
 
-        for s in range(2):
-            for i, count, o_mean, o_spread in ((s, CLASSES, o_cm, o_cs), (2 + s, levels, o_dm, o_ds)):
-                part = [final[de, at[i] : at[i + 1], :] for de in range(members)]
-                mean = sum(part[1:], part[0]) / members
-                square = [jnp.square(x - mean) for x in part]
-                spread = jnp.sqrt(sum(square[1:], square[0]) / (members - 1))
-                for r in range(REGIONS):
-                    o_mean[0, r, s] = mean[:count, r * rows : (r + 1) * rows]
-                    o_spread[0, r, s] = spread[:count, r * rows : (r + 1) * rows]
-
         for t in range(devices - 1):
             table_copy(t).wait_send()
         for copy in copies + tails:
             copy.wait_send()
 
-    out = lambda n: jax.ShapeDtypeStruct((1, REGIONS, 2, n, rows), F32)
     slots = max(1, devices - 1)
     dma = pltpu.SemaphoreType.DMA
     return pl.pallas_call(
         kernel,
-        out_shape=[out(levels), out(levels), out(CLASSES), out(CLASSES)],
+        out_shape=jax.ShapeDtypeStruct((members, tall, lanes), F32),
         in_specs=[pl.BlockSpec(memory_space=pl.ANY)] * 5,
-        out_specs=[pl.BlockSpec(memory_space=pltpu.VMEM)] * 4,
+        out_specs=pl.BlockSpec(memory_space=pltpu.VMEM),
         scratch_shapes=const_shapes(sz, lons)
         + work_shapes(sz, lons)
         + [
@@ -386,7 +375,6 @@
             pltpu.VMEM((members - 1, tall, lanes), F32),
             pltpu.VMEM((2 * SUB, ends), F32),
             pltpu.VMEM((len(far), 2 * SUB, ends), F32),
-            pltpu.VMEM((members, tall, lanes), F32),
             dma((devices, 3)),
             dma((2,)),
             dma((slots,)),
@@ -402,10 +390,37 @@
     )(north_vel, up_vel, dens_class, thickness, basin_id)
 
 
+def moments(sz, final):
+    members = final.shape[0]
+    at, rows, levels, lanes = table_rows(sz), sz["rows"], sz["levels"], sz["lanes"]
+
+    def kernel(final, o_dm, o_ds, o_cm, o_cs):
+        for s in range(2):
+            for i, count, o_mean, o_spread in ((s, CLASSES, o_cm, o_cs), (2 + s, levels, o_dm, o_ds)):
+                part = [final[de, at[i] : at[i + 1], :] for de in range(members)]
+                mean = sum(part[1:], part[0]) / members
+                square = [jnp.square(x - mean) for x in part]
+                spread = jnp.sqrt(sum(square[1:], square[0]) / (members - 1))
+                for o, x in ((o_mean, mean), (o_spread, spread)):
+                    pad = round_up(x.shape[0], 128) - x.shape[0]
+                    x = jnp.concatenate([x, jnp.zeros((pad, lanes), F32)], 0).T
+                    for r in range(REGIONS):
+                        o[0, r, s] = x[r * rows : (r + 1) * rows, :count]
+
+    out = lambda n: jax.ShapeDtypeStruct((1, REGIONS, 2, rows, n), F32)
+    outs = pl.pallas_call(
+        kernel,
+        out_shape=[out(levels), out(levels), out(CLASSES), out(CLASSES)],
+        in_specs=[pl.BlockSpec(memory_space=pltpu.VMEM)],
+        out_specs=[pl.BlockSpec(memory_space=pltpu.VMEM)] * 4,
+    )(final)
+    return tuple(jnp.swapaxes(x, 3, 4) for x in outs)
+
+
 def body(north_vel, up_vel, dens_class, thickness, basin_id):
     levels, rows = north_vel.shape[2:4]
     sz = sizes_of(levels, rows)
-    return tuple(fused(sz, north_vel, up_vel, dens_class, thickness, basin_id))
+    return moments(sz, fused(sz, north_vel, up_vel, dens_class, thickness, basin_id))
 
 
 def solution(mesh):

time: 60.7 us -> 43.2 us (0.71)
  Pallas kernels: 52.7 us -> 42.4 us
  local copies, waits for them, and re-layouts: 7.08 us -> 0 us
    pallas_call x1 -> x2, Pallas kernels: 52.7 us -> 42.4 us  [the longest x1 40.4 us: fused(): pl.pallas_call(kernel, out_shape=jax.ShapeDtypeStruct((members, tall, lan...]
    pallas_call x4 -> x0, local copies, waits for them, and re-layouts: 7.08 us -> none  [fused(): pl.pallas_call(kernel, out_shape=[out(levels), out(levels), out(CLASSES),...]
where the time goes in v3:
time: 43.2 us; the launch traced here: 43 us
  Pallas kernels  42.4 us (98%)
  between operations  0.64 us (1%)
    pallas_call x1, Pallas kernels, fused(): pl.pallas_call(kernel, out_shape=jax.ShapeDtypeStruct((members, tall, lan...  40.4 us
    pallas_call x1, Pallas kernels, moments(): pl.pallas_call(kernel, out_shape=[out(levels), out(levels), out(CLASSES),...  1.95 us

profile of v3, /device:TPU:0, one launch (start us, length us, event | category | flops | bytes accessed | tf_op | source)
XLA Modules:
  0.0 43.0 jit_solution(8957150625518283818)
XLA Ops:
  0.6 40.4 %shard_map.84.final = f32[2,320,128]{2,1,0:T(8,128)} custom-call(bf16[1,4,75,32,128]{4,3,2,1,0:T(8,128)(2,1)} %north_h.1, bf16[1,4,75,32,128]{4,3,2,1,0:T(8,128)(2,1)} %up_h.1, s32[1,4,75,32,128]{4,3,2,1,0:T(8,128)} %dens_h.1, s32[75,32,128]{2,1,0:T(8,128)} %thick_h.1, s32[32,128]{1,0:T(8,128)} %basin_h.1), custom_call_target="tpu_custom_call" | custom-call | tf_op jit(solution)/shard_map/pallas_call | solution.py:358
  41.1 1.9 %shard_map.85 = (f32[1,4,2,32,75]{4,3,2,1,0:T(8,128)}, f32[1,4,2,32,75]{4,3,2,1,0:T(8,128)}, f32[1,4,2,32,80]{4,3,2,1,0:T(8,128)}, f32[1,4,2,32,80]{4,3,2,1,0:T(8,128)}) custom-call(f32[2,320,128]{2,1,0:T(8,128)} %shard_map.84.final), custom_call_target="tpu_custom_call" | custom-call | tf_op jit(solution)/shard_map/pallas_call | solution.py:411
